TPU v7x, 32 devices: a whole 2x2x4 slice. The times are simulated.
32 devices in a mesh: dp: 8 (over y, x, core), tensor: 4 (over z).
Axes of the slice: x: 2, y: 2, z: 4, core: 2. Of those that a mesh axis runs over, the one named last changes fastest.
Arguments:
- tokens: bfloat16 [16384, 768], P('dp'), may hold values from -6 to 6
- doc_lengths: int32 [16, 8], P('dp'), may hold values from 1 to 512, 1024 in all within a row
- wq: bfloat16 [768, 768], P('dp', 'tensor'), may hold values from -0.21875 to 0.21875
- bq: float32 [768], P('tensor'), may hold values from -3 to 3
- wk: bfloat16 [768, 768], P('dp', 'tensor'), may hold values from -0.21875 to 0.21875
- wv: bfloat16 [768, 768], P('dp', 'tensor'), may hold values from -0.21875 to 0.21875
- bv: float32 [768], P('tensor'), may hold values from -3 to 3
- wo: bfloat16 [768, 768], P('tensor', 'dp'), may hold values from -0.875 to 0.875
- bo: float32 [768], replicated, may hold values from -3 to 3
- gain1: float32 [768], replicated, may hold values from 0.25 to 1.75
- shift1: float32 [768], replicated, may hold values from -3 to 3
- w1: bfloat16 [768, 3072], P('dp', 'tensor'), may hold values from -0.21875 to 0.21875
- b1: float32 [3072], P('tensor'), may hold values from -3 to 3
- w2: bfloat16 [3072, 768], P('tensor', 'dp'), may hold values from -0.109375 to 0.109375
- b2: float32 [768], replicated, may hold values from -3 to 3
- gain2: float32 [768], replicated, may hold values from 0.25 to 1.75
- shift2: float32 [768], replicated, may hold values from -3 to 3
- cotangent: bfloat16 [16384, 768], P('dp'), may hold values from -6 to 6
Outputs:
- out: bfloat16 [16384, 768], P('dp')
- grad_tokens: bfloat16 [16384, 768], P('dp')
- grad_wq: float32 [768, 768], P('dp', 'tensor')
- grad_bq: float32 [768], P('tensor')
- grad_wk: float32 [768, 768], P('dp', 'tensor')
- grad_wv: float32 [768, 768], P('dp', 'tensor')
- grad_bv: float32 [768], P('tensor')
- grad_wo: float32 [768, 768], P('tensor', 'dp')
- grad_bo: float32 [768], replicated
- grad_gain1: float32 [768], replicated
- grad_shift1: float32 [768], replicated
- grad_w1: float32 [768, 3072], P('dp', 'tensor')
- grad_b1: float32 [3072], P('tensor')
- grad_w2: float32 [3072, 768], P('tensor', 'dp')
- grad_b2: float32 [768], replicated
- grad_gain2: float32 [768], replicated
- grad_shift2: float32 [768], replicated
Inputs may be any that keep to these rules, and one draw needn't show every extreme that they name: `doc_lengths`: row s holds the lengths of the documents packed in order into sequence s; each row sums to 1024.
All inputs are finite; a program needn't handle non-finite values.
Results may differ from a plain program's by a relative error of at most 0.02.
Values may be sent and summed in bfloat16 or wider, within the bound.
A program may use at most 192 MiB of HBM per device.

v0:
```python
from functools import partial
import jax
import jax.numpy as jnp
from jax import lax
from jax.sharding import PartitionSpec as P

HD = 64
eps_norm = 1e-12
masked_score = -1e30


def doc_ids(lengths, count):
    ends = jnp.cumsum(lengths)
    places = jnp.arange(count, dtype=jnp.int32)
    return jnp.sum((places[:, None] >= ends[None, :]).astype(jnp.int32), axis=1)


def collect(wq, wk, wv, wo, w1, w2):
    return (
        lax.all_gather(wq, "dp", axis=0, tiled=True),
        lax.all_gather(wk, "dp", axis=0, tiled=True),
        lax.all_gather(wv, "dp", axis=0, tiled=True),
        lax.all_gather(wo, "dp", axis=1, tiled=True),
        lax.all_gather(w1, "dp", axis=0, tiled=True),
        lax.all_gather(w2, "dp", axis=1, tiled=True),
    )


def reduce_large(grads):
    return (
        lax.psum_scatter(grads[0], "dp", scatter_dimension=0, tiled=True),
        lax.psum_scatter(grads[1], "dp", scatter_dimension=0, tiled=True),
        lax.psum_scatter(grads[2], "dp", scatter_dimension=0, tiled=True),
        lax.psum_scatter(grads[3], "dp", scatter_dimension=1, tiled=True),
        lax.psum_scatter(grads[4], "dp", scatter_dimension=0, tiled=True),
        lax.psum_scatter(grads[5], "dp", scatter_dimension=1, tiled=True),
    )


def reduce_small(grads):
    return lax.psum(
        (grads[0], grads[1], grads[2], grads[3], grads[4], grads[5], grads[6], grads[7], grads[8]),
        "dp",
    )


def contract_rows(left, right):
    return lax.dot_general(
        left, right, (((0,), (0,)), ((), ())), preferred_element_type=jnp.float32
    )


def contract_cols(left, right):
    return lax.dot_general(
        left, right, (((1,), (1,)), ((), ())), preferred_element_type=jnp.float32
    )


def contract_mixed(left, right):
    return lax.dot_general(
        left, right, (((0,), (1,)), ((), ())), preferred_element_type=jnp.float32
    )


def norm_forward(total, gain, shift):
    centre = total - jnp.mean(total, axis=-1, keepdims=True)
    scaled = lax.rsqrt(jnp.mean(centre * centre, axis=-1, keepdims=True) + eps_norm)
    normed = centre * scaled
    return (normed * gain + shift, normed, scaled)


def norm_backward(grad_result, normed, scaled, gain):
    grad_normed = grad_result * gain
    mean_grad = jnp.mean(grad_normed, axis=-1, keepdims=True)
    mean_cross = jnp.mean(grad_normed * normed, axis=-1, keepdims=True)
    grad_total = scaled * (grad_normed - mean_grad - normed * mean_cross)
    return (grad_total, jnp.sum(grad_result * normed, axis=0), jnp.sum(grad_result, axis=0))


def block_scores(query_block, key_heads, seg_block, seg, scale):
    raw = (
        jnp.einsum("hdq,hdk->hqk", query_block, key_heads, preferred_element_type=jnp.float32)
        * scale
    )
    same_doc = seg_block[:, None] == seg[None, :]
    return jnp.where(same_doc[None], raw, masked_score)


def body(
    tokens,
    doc_lengths,
    wq,
    bq,
    wk,
    wv,
    bv,
    wo,
    bo,
    gain1,
    shift1,
    w1,
    b1,
    w2,
    b2,
    gain2,
    shift2,
    cotangent,
):
    micro = doc_lengths.shape[0]
    seq_len = tokens.shape[0] // micro
    block = min(512, seq_len)
    scale = HD ** (-0.5)
    results = []
    grad_inputs = []
    large_total = None
    small_total = None
    for index in range(micro):
        full = collect(wq, wk, wv, wo, w1, w2)
        full_q, full_k, full_v, full_o, full_first, full_second = full
        width = full_q.shape[1]
        heads_here = width // HD
        rows_in = tokens[index * seq_len : (index + 1) * seq_len]
        inputs = rows_in.astype(jnp.float32)
        seg = doc_ids(doc_lengths[index], seq_len)
        queries = (
            lax.dot_general(
                full_q, rows_in, (((0,), (1,)), ((), ())), preferred_element_type=jnp.float32
            )
            + bq[:, None]
        ).astype(jnp.bfloat16)
        keys_low = lax.dot_general(
            full_k, rows_in, (((0,), (1,)), ((), ())), preferred_element_type=jnp.float32
        ).astype(jnp.bfloat16)
        values_low = (
            lax.dot_general(
                full_v, rows_in, (((0,), (1,)), ((), ())), preferred_element_type=jnp.float32
            )
            + bv[:, None]
        ).astype(jnp.bfloat16)
        query_heads = queries.reshape(heads_here, HD, seq_len)
        key_heads = keys_low.reshape(heads_here, HD, seq_len)
        value_heads = values_low.reshape(heads_here, HD, seq_len)
        pieces = []
        log_totals = []
        for offset in range(0, seq_len, block):
            scores = block_scores(
                query_heads[:, :, offset : offset + block],
                key_heads,
                seg[offset : offset + block],
                seg,
                scale,
            )
            highest = jnp.max(scores, axis=-1, keepdims=True)
            log_total = highest + jnp.log(
                jnp.sum(jnp.exp(scores - highest), axis=-1, keepdims=True)
            )
            probs_low = jnp.exp(scores - log_total).astype(jnp.bfloat16)
            pieces.append(
                jnp.einsum(
                    "hqk,hdk->hdq", probs_low, value_heads, preferred_element_type=jnp.float32
                )
            )
            log_totals.append(log_total)
        mixed_cols = jnp.concatenate(pieces, axis=2).reshape(width, seq_len).astype(jnp.bfloat16)
        attended = lax.psum(
            contract_rows(mixed_cols, full_o).astype(jnp.bfloat16), "tensor"
        ).astype(jnp.float32)
        first, normed_one, scaled_one = norm_forward(inputs + attended + bo, gain1, shift1)
        first_low = first.astype(jnp.bfloat16)
        inner = jnp.dot(first_low, full_first, preferred_element_type=jnp.float32) + b1
        hidden = jax.nn.gelu(inner, approximate=False).astype(jnp.bfloat16)
        second = lax.psum(
            jnp.dot(hidden, full_second, preferred_element_type=jnp.float32).astype(jnp.bfloat16),
            "tensor",
        ).astype(jnp.float32)
        result, normed_two, scaled_two = norm_forward(first + second + b2, gain2, shift2)
        results.append(result.astype(jnp.bfloat16))
        grad_result = cotangent[index * seq_len : (index + 1) * seq_len].astype(jnp.float32)
        grad_two, grad_gain2, grad_shift2 = norm_backward(
            grad_result, normed_two, scaled_two, gain2
        )
        grad_b2 = jnp.sum(grad_two, axis=0)
        full = collect(wq, wk, wv, wo, w1, w2)
        full_q, full_k, full_v, full_o, full_first, full_second = full
        two_low = grad_two.astype(jnp.bfloat16)
        grad_w2 = contract_rows(hidden, two_low)
        grad_hidden = contract_cols(two_low, full_second)
        grad_inner = jax.vjp(partial(jax.nn.gelu, approximate=False), inner)[1](grad_hidden)[
            0
        ].astype(jnp.bfloat16)
        grad_b1 = jnp.sum(grad_inner.astype(jnp.float32), axis=0)
        grad_w1 = contract_rows(first_low, grad_inner)
        grad_first = grad_two + lax.psum(
            contract_cols(grad_inner, full_first).astype(jnp.bfloat16), "tensor"
        ).astype(jnp.float32)
        grad_one, grad_gain1, grad_shift1 = norm_backward(grad_first, normed_one, scaled_one, gain1)
        grad_bo = jnp.sum(grad_one, axis=0)
        one_low = grad_one.astype(jnp.bfloat16)
        grad_wo = jnp.dot(mixed_cols, one_low, preferred_element_type=jnp.float32)
        grad_mixed = (
            contract_cols(full_o, one_low).astype(jnp.bfloat16).reshape(heads_here, HD, seq_len)
        )
        grad_key_heads = jnp.zeros((heads_here, HD, seq_len), jnp.float32)
        grad_value_heads = jnp.zeros((heads_here, HD, seq_len), jnp.float32)
        grad_query_pieces = []
        for number, offset in enumerate(range(0, seq_len, block)):
            query_block = query_heads[:, :, offset : offset + block]
            grad_block = grad_mixed[:, :, offset : offset + block]
            scores = block_scores(query_block, key_heads, seg[offset : offset + block], seg, scale)
            probs = jnp.exp(scores - log_totals[number])
            grad_probs = jnp.einsum(
                "hdq,hdk->hqk", grad_block, value_heads, preferred_element_type=jnp.float32
            )
            centre = jnp.sum(probs * grad_probs, axis=-1, keepdims=True)
            grad_scores = (probs * (grad_probs - centre)).astype(jnp.bfloat16)
            grad_query_pieces.append(
                jnp.einsum(
                    "hqk,hdk->hdq", grad_scores, key_heads, preferred_element_type=jnp.float32
                )
                * scale
            )
            grad_key_heads = (
                grad_key_heads
                + jnp.einsum(
                    "hqk,hdq->hdk", grad_scores, query_block, preferred_element_type=jnp.float32
                )
                * scale
            )
            grad_value_heads = grad_value_heads + jnp.einsum(
                "hqk,hdq->hdk",
                probs.astype(jnp.bfloat16),
                grad_block,
                preferred_element_type=jnp.float32,
            )
        grad_queries = (
            jnp.concatenate(grad_query_pieces, axis=2).reshape(width, seq_len).astype(jnp.bfloat16)
        )
        grad_keys = grad_key_heads.reshape(width, seq_len).astype(jnp.bfloat16)
        grad_values = grad_value_heads.reshape(width, seq_len).astype(jnp.bfloat16)
        grad_bq = jnp.sum(grad_queries.astype(jnp.float32), axis=1)
        grad_bv = jnp.sum(grad_values.astype(jnp.float32), axis=1)
        grad_wq = contract_cols(rows_in.T, grad_queries)
        grad_wk = contract_cols(rows_in.T, grad_keys)
        grad_wv = contract_cols(rows_in.T, grad_values)
        back_terms = (
            contract_mixed(grad_queries, full_q)
            + contract_mixed(grad_keys, full_k)
            + contract_mixed(grad_values, full_v)
        )
        grad_rows = grad_one + lax.psum(back_terms.astype(jnp.bfloat16), "tensor").astype(
            jnp.float32
        )
        grad_inputs.append(grad_rows.astype(jnp.bfloat16))
        large_local = (grad_wq, grad_wk, grad_wv, grad_wo, grad_w1, grad_w2)
        small_local = (
            grad_bq,
            grad_bv,
            grad_b1,
            grad_bo,
            grad_b2,
            grad_gain1,
            grad_shift1,
            grad_gain2,
            grad_shift2,
        )
        large_local = reduce_large(large_local)
        small_local = reduce_small(small_local)
        if large_total is None:
            large_total = large_local
            small_total = small_local
        else:
            large_total = jax.tree.map(jnp.add, large_total, large_local)
            small_total = jax.tree.map(jnp.add, small_total, small_local)
    grad_wq, grad_wk, grad_wv, grad_wo, grad_w1, grad_w2 = large_total
    (
        grad_bq,
        grad_bv,
        grad_b1,
        grad_bo,
        grad_b2,
        grad_gain1,
        grad_shift1,
        grad_gain2,
        grad_shift2,
    ) = small_total
    return (
        jnp.concatenate(results, axis=0),
        jnp.concatenate(grad_inputs, axis=0),
        grad_wq,
        grad_bq,
        grad_wk,
        grad_wv,
        grad_bv,
        grad_wo,
        grad_bo,
        grad_gain1,
        grad_shift1,
        grad_w1,
        grad_b1,
        grad_w2,
        grad_b2,
        grad_gain2,
        grad_shift2,
    )


def solution(mesh):
    placed = (
        P("dp", None),
        P("dp", None),
        P("dp", "tensor"),
        P("tensor"),
        P("dp", "tensor"),
        P("dp", "tensor"),
        P("tensor"),
        P("tensor", "dp"),
        P(),
        P(),
        P(),
        P("dp", "tensor"),
        P("tensor"),
        P("tensor", "dp"),
        P(),
        P(),
        P(),
        P("dp", None),
    )
    return jax.shard_map(
        body,
        mesh=mesh,
        in_specs=placed,
        out_specs=(
            P("dp", None),
            P("dp", None),
            P("dp", "tensor"),
            P("tensor"),
            P("dp", "tensor"),
            P("dp", "tensor"),
            P("tensor"),
            P("tensor", "dp"),
            P(),
            P(),
            P(),
            P("dp", "tensor"),
            P("tensor"),
            P("tensor", "dp"),
            P(),
            P(),
            P(),
        ),
        check_vma=False,
    )
```

profile of v0, /device:TPU:0, one launch (start us, length us, event | category | flops | bytes accessed | tf_op | source)
XLA Modules:
  0.0 842.3 jit_solution(16882995216697023067)
XLA Ops:
  8.1 11.6 %all_gather.12 = bf16[768,192]{1,0:T(8,128)(2,1)S(1)} all-gather(bf16[96,192]{1,0:T(8,128)(2,1)} %param.23), channel_id=1, replica_groups=mesh['dp'=8,'tensor'=4] {'dp'}, dimensions={0}, use_global_device_ids=true | all-gather | bytes 331776 | tf_op jit(solution)/shard_map/all_gather | solution.py:22
  24.1 9.4 %all_gather.14 = bf16[768,192]{1,0:T(8,128)(2,1)S(1)} all-gather(bf16[96,192]{1,0:T(8,128)(2,1)S(1)} %copy-done.92), channel_id=1, replica_groups=mesh['dp'=8,'tensor'=4] {'dp'}, dimensions={0}, use_global_device_ids=true | all-gather | bytes 331776 | tf_op jit(solution)/shard_map/all_gather | solution.py:21
  36.5 9.0 %all_gather.13 = bf16[768,192]{1,0:T(8,128)(2,1)S(1)} all-gather(bf16[96,192]{1,0:T(8,128)(2,1)S(1)} %copy-done.93), channel_id=1, replica_groups=mesh['dp'=8,'tensor'=4] {'dp'}, dimensions={0}, use_global_device_ids=true | all-gather | bytes 331776 | tf_op jit(solution)/shard_map/all_gather | solution.py:20
  50.2 9.3 %all_gather.15 = bf16[192,768]{0,1:T(8,128)(2,1)S(1)} all-gather(bf16[192,96]{0,1:T(8,128)(2,1)} %copy.42), channel_id=1, replica_groups=mesh['dp'=8,'tensor'=4] {'dp'}, dimensions={1}, use_global_device_ids=true | all-gather | bytes 331776 | tf_op jit(solution)/shard_map/all_gather | solution.py:23
  90.3 120.7 %all-reduce.16.cloned.1.call-done = (bf16[1024,768]{1,0:T(8,128)(2,1)}, bf16[1024,768]{1,0:T(8,128)(2,1)}) async-done(((bf16[1024,768]{1,0:T(8,128)(2,1)}, bf16[1024,768]{1,0:T(8,128)(2,1)}), (bf16[1024,768]{1,0:T(8,128)(2,1)}, bf16[1024,768]{1,0:T(8,128)(2,1)})) %all-reduce.16.cloned.1.call-update) | async-done | bytes 3145744 | tf_op jit(solution)/shard_map/psum | solution.py:165
  216.2 3.8 fusion.68
  221.7 17.1 %multiply_convert_fusion.5 = (bf16[1024,768]{1,0:T(8,128)(2,1)}, f32[1024,768]{1,0:T(8,128)}, bf16[1024,768]{1,0:T(8,128)(2,1)}, f32[1024,768]{1,0:T(8,128)}, f32[1024,768]{1,0:T(8,128)}) fusion(f32[768]{0:T(1024)S(1)} %copy-done.119, f32[1024,768]{1,0:T(8,128)S(1)} %fusion.68, bf16[768,768]{1,0:T(8,128)(2,1)S(1)} %copy-done.115, f32[768]{0:T(1024)S(1)} %copy-done.110, ...), kind=kOutput, calls=%fused_computation.92 | convolution fusion | flops 1318846464 | bytes 20078592 | tf_op jit(solution)/shard_map/dot_general | solution.py:170
  238.9 4.5 convolution_convert_fusion.4
  246.0 120.6 %all-reduce.14.cloned.1.call-done = (bf16[1024,768]{1,0:T(8,128)(2,1)}, bf16[1024,768]{1,0:T(8,128)(2,1)}) async-done(((bf16[1024,768]{1,0:T(8,128)(2,1)}, bf16[1024,768]{1,0:T(8,128)(2,1)}), (bf16[1024,768]{1,0:T(8,128)(2,1)}, bf16[1024,768]{1,0:T(8,128)(2,1)})) %all-reduce.14.cloned.1.call-update) | async-done | bytes 3145744 | tf_op jit(solution)/shard_map/psum | solution.py:172
  366.5 5.4 fusion.131
  377.4 4.3 fusion.18
  395.3 120.6 %all-reduce.12.cloned.1.call-done = (bf16[1024,768]{1,0:T(8,128)(2,1)}, bf16[1024,768]{1,0:T(8,128)(2,1)}) async-done(((bf16[1024,768]{1,0:T(8,128)(2,1)}, bf16[1024,768]{1,0:T(8,128)(2,1)}), (bf16[1024,768]{1,0:T(8,128)(2,1)}, bf16[1024,768]{1,0:T(8,128)(2,1)})) %all-reduce.12.cloned.1.call-update) | async-done | bytes 3145744 | tf_op jit(solution)/shard_map/psum | solution.py:193
  515.9 9.4 %multiply_reduce_fusion.5 = (f32[768]{0:T(1024)}, f32[1024]{0:T(1024)S(1)}, f32[1024]{0:T(1024)S(1)}, f32[768]{0:T(1024)}, f32[768]{0:T(1024)}, /*index=5*/f32[1...) fusion(f32[1024,768]{1,0:T(8,128)} %copy-done.18, bf16[1024,768]{1,0:T(8,128)(2,1)} %get-tuple-element.110, ...), kind=kLoop, calls=%fused_computation.57 | loop fusion | flops 24371456 | bytes 15782912 | tf_op jit(solution)/shard_map/reduce_sum | solution.py:77
  525.4 5.3 fusion.130
  537.4 4.4 multiply_reduce_fusion
  541.8 4.3 multiply_reduce_fusion.1
  546.1 8.4 multiply_convert_fusion
  554.6 3.8 convolution_multiply_fusion.1
  560.1 5.7 fusion.84
  565.9 4.4 multiply_reduce_fusion.2
  570.3 4.4 multiply_reduce_fusion.3
  574.7 8.2 multiply_convert_fusion.2
  582.9 3.8 convolution_multiply_fusion.3
  592.4 5.8 convert_reduce_fusion.4
  598.2 5.6 convert_reduce_fusion.5
  616.7 4.0 fusion.61
  623.9 4.0 fusion.70
  656.6 26.5 %all-reduce = (f32[192]{0:T(256)}, f32[192]{0:T(256)}, f32[768]{0:T(1024)}, f32[768]{0:T(1024)}, f32[768]{0:T(1024)}, /*index=5*/f32[768]{0:T(1024)}, f32[768]{0:T(1024)}, f32[768]{0:T(1024)}, f32[768]{0:T(1024)}) all-reduce(f32[192]{0:T(256)} %reshape.371, f32[192]{0:T(256)} %reshape.372, ...), channel_id=1, replica_groups=mesh['dp'=8,'tensor'=4] {'dp'}, use_global_device_ids=true, to_apply=%region_43.44 | all-reduce | flops 5760 | bytes 46080 | tf_op jit(solution)/shard_map/psum | solution.py:41
  684.8 52.3 %all-reduce.10.cloned.1.call-done = (bf16[1024,768]{1,0:T(8,128)(2,1)}, bf16[1024,768]{1,0:T(8,128)(2,1)}) async-done(((bf16[1024,768]{1,0:T(8,128)(2,1)}, bf16[1024,768]{1,0:T(8,128)(2,1)}), (bf16[1024,768]{1,0:T(8,128)(2,1)}, bf16[1024,768]{1,0:T(8,128)(2,1)})) %all-reduce.10.cloned.1.call-update) | async-done | bytes 3145744 | tf_op jit(solution)/shard_map/psum | solution.py:250
  743.1 14.7 %reduce-scatter.23.cloned.1.call-done = f32[96,192]{1,0:T(8,128)} async-done(((f32[768,192]{1,0:T(8,128)}), f32[96,192]{1,0:T(8,128)}) %reduce-scatter.23.cloned.1.call-update) | async-done | bytes 73744
  757.8 38.6 %reduce-scatter.19.cloned.1.call-done = f32[96,192]{1,0:T(8,128)} async-done(((f32[768,192]{1,0:T(8,128)}), f32[96,192]{1,0:T(8,128)}) %reduce-scatter.19.cloned.1.call-update) | async-done | bytes 73744
  796.4 38.6 %reduce-scatter.21.cloned.1.call-done = f32[96,192]{1,0:T(8,128)} async-done(((f32[768,192]{1,0:T(8,128)}), f32[96,192]{1,0:T(8,128)}) %reduce-scatter.21.cloned.1.call-update) | async-done | bytes 73744
  (427 shorter events, 136.9 us)
Async XLA Ops:
  8.0 14.6 %copy-start = (bf16[2048,768]{1,0:T(8,128)(2,1)S(1)}, bf16[2048,768]{1,0:T(8,128)(2,1)}, u32[]{:S(2)}) copy-start(bf16[2048,768]{1,0:T(8,128)(2,1)} %param.18) | copy-start | bytes 9437188
  8.0 14.6 %copy-start.121 = (f32[192]{0:T(256)S(1)}, f32[192]{0:T(256)}, u32[]{:S(2)}) copy-start(f32[192]{0:T(256)} %param.24) | copy-start | bytes 2308
  8.0 16.1 %copy-start.92 = (bf16[96,192]{1,0:T(8,128)(2,1)S(1)}, bf16[96,192]{1,0:T(8,128)(2,1)}, u32[]{:S(2)}) copy-start(bf16[96,192]{1,0:T(8,128)(2,1)} %param.22) | copy-start | bytes 110596
  8.1 202.9 %all-reduce.16.cloned.1.call-start = ((), (), s32[]{:S(2)}) async-start(), calls=%async_computation.17 | async-start | bytes 6291456 | tf_op jit(solution)/shard_map/psum | solution.py:165
  19.7 13.9 %copy-start.40 = (bf16[768,192]{1,0:T(8,128)(2,1)}, bf16[768,192]{1,0:T(8,128)(2,1)S(1)}, u32[]{:S(2)}) copy-start(bf16[768,192]{1,0:T(8,128)(2,1)S(1)} %all_gather.12) | copy-start | bytes 884740
  24.1 12.3 %copy-start.93 = (bf16[96,192]{1,0:T(8,128)(2,1)S(1)}, bf16[96,192]{1,0:T(8,128)(2,1)}, u32[]{:S(2)}) copy-start(bf16[96,192]{1,0:T(8,128)(2,1)} %param.20) | copy-start | bytes 110596
  24.1 21.3 %copy-start.122 = (f32[192]{0:T(256)S(1)}, f32[192]{0:T(256)}, u32[]{:S(2)}) copy-start(f32[192]{0:T(256)} %param.21) | copy-start | bytes 2308
  33.6 13.3 %copy-start.52 = (bf16[768,192]{1,0:T(8,128)(2,1)}, bf16[768,192]{1,0:T(8,128)(2,1)S(1)}, u32[]{:S(2)}) copy-start(bf16[768,192]{1,0:T(8,128)(2,1)S(1)} %all_gather.14) | copy-start | bytes 884740
  36.4 11.9 %copy-start.114 = (s32[2,8]{1,0:T(2,128)S(1)}, s32[2,8]{1,0:T(2,128)}, u32[]{:S(2)}) copy-start(s32[2,8]{1,0:T(2,128)} %param.19) | copy-start | bytes 196
  36.5 13.0 %copy-start.94 = (bf16[192,96]{1,0:T(8,128)(2,1)S(1)}, bf16[192,96]{1,0:T(8,128)(2,1)}, u32[]{:S(2)}) copy-start(bf16[192,96]{1,0:T(8,128)(2,1)} %param.25) | copy-start | bytes 110596
  60.9 10.0 %copy-start.24 = (pred[512,1024]{1,0:T(8,128)(4,1)}, pred[512,1024]{1,0:T(8,128)(4,1)S(1)}, u32[]{:S(2)}) copy-start(pred[512,1024]{1,0:T(8,128)(4,1)S(1)} %get-tuple-element.151) | copy-start | bytes 1572868
  86.5 124.5 %copy-start.78 = (f32[768]{0:T(1024)S(1)}, f32[768]{0:T(1024)}, u32[]{:S(2)}) copy-start(f32[768]{0:T(1024)} %param.26) | copy-start | bytes 9220
  89.1 127.1 %all-gather.3.cloned.1.call-start = ((), (), s32[]{:S(2)}) async-start(), calls=%async_computation.6 | async-start | bytes 1327104 | tf_op jit(solution)/shard_map/all_gather | solution.py:24
  89.7 149.2 %all-gather.5.cloned.1.call-start = ((), (), s32[]{:S(2)}) async-start(), calls=%async_computation.7 | async-start | bytes 1327104 | tf_op jit(solution)/shard_map/all_gather | solution.py:25
  90.3 276.3 %all-reduce.14.cloned.1.call-start = ((), (), s32[]{:S(2)}) async-start(), calls=%async_computation.16 | async-start | bytes 6291456 | tf_op jit(solution)/shard_map/psum | solution.py:172
  245.9 269.9 %all-reduce.12.cloned.1.call-start = ((), (), s32[]{:S(2)}) async-start(), calls=%async_computation.15 | async-start | bytes 6291456 | tf_op jit(solution)/shard_map/psum | solution.py:193
  395.2 287.9 %reduce-scatter.25.cloned.1.call-start = ((), (), s32[]{:S(2)}) async-start(), calls=%async_computation.13 | async-start | bytes 884736
  515.8 9.5 %copy-start.90 = (f32[1024]{0:T(1024)S(1)}, f32[1024]{0:T(1024)}, u32[]{:S(2)}) copy-start(f32[1024]{0:T(1024)} %add_rsqrt_fusion.1) | copy-start | bytes 12292
  515.9 9.5 %copy-start.96 = (f32[768]{0:T(1024)S(1)}, f32[768]{0:T(1024)}, u32[]{:S(2)}) copy-start(f32[768]{0:T(1024)} %param.27) | copy-start | bytes 9220
  515.9 18.7 %slice-start.4 = ((s8[6291456]{0:T(1024)(128)(4,1)}), s8[4194304]{0:T(1024)(128)(4,1)S(1)}, s32[]{:S(2)}) async-start(s8[6291456]{0:T(1024)(128)(4,1)} %bitcast.113), calls=%async_computation.22 | async-start | bytes 8388608
  546.1 12.3 %copy-start.63 = (bf16[192,1024]{1,0:T(8,128)(2,1)S(1)}, bf16[192,1024]{1,0:T(8,128)(2,1)}, u32[]{:S(2)}) copy-start(bf16[192,1024]{1,0:T(8,128)(2,1)} %fusion.50) | copy-start | bytes 1179652
  546.1 13.9 %copy-start.88 = (f32[3,512]{1,0:T(4,128)S(1)}, f32[3,512]{1,0:T(4,128)}, u32[]{:S(2)}) copy-start(f32[3,512]{1,0:T(4,128)} %copy-done.87) | copy-start | bytes 18436
  554.6 11.2 %slice-start.2 = ((s8[6291456]{0:T(1024)(128)(4,1)}), s8[4194304]{0:T(1024)(128)(4,1)S(1)}, s32[]{:S(2)}) async-start(s8[6291456]{0:T(1024)(128)(4,1)} %bitcast.111), calls=%async_computation.20 | async-start | bytes 8388608
  560.1 10.2 %slice-start.6 = ((s8[6291456]{0:T(1024)(128)(4,1)}), s8[4194304]{0:T(1024)(128)(4,1)S(1)}, s32[]{:S(2)}) async-start(s8[6291456]{0:T(1024)(128)(4,1)} %bitcast.115), calls=%async_computation.24 | async-start | bytes 8388608
  591.9 145.2 %all-reduce.10.cloned.1.call-start = ((), (), s32[]{:S(2)}) async-start(), calls=%async_computation.14 | async-start | bytes 6291456 | tf_op jit(solution)/shard_map/psum | solution.py:250
  598.2 14.5 %copy-start.57 = (bf16[3,64,1024]{2,1,0:T(8,128)(2,1)}, bf16[3,64,1024]{2,1,0:T(8,128)(2,1)S(1)}, u32[]{:S(2)}) copy-start(bf16[3,64,1024]{2,1,0:T(8,128)(2,1)S(1)} %get-tuple-element.176) | copy-start | bytes 1179652
  603.8 10.8 %copy-start.77 = (bf16[3,64,1024]{2,1,0:T(8,128)(2,1)}, bf16[3,64,1024]{2,1,0:T(8,128)(2,1)S(1)}, u32[]{:S(2)}) copy-start(bf16[3,64,1024]{2,1,0:T(8,128)(2,1)S(1)} %get-tuple-element.174) | copy-start | bytes 1179652
  616.5 126.7 %reduce-scatter.17.cloned.1.call-start = ((), (), s32[]{:S(2)}) async-start(), calls=%async_computation.9 | async-start | bytes 2654208 | tf_op jit(solution)/shard_map/reduce_scatter | solution.py:36
  623.8 119.4 %reduce-scatter.15.cloned.1.call-start = ((), (), s32[]{:S(2)}) async-start(), calls=%async_computation.8 | async-start | bytes 2654208 | tf_op jit(solution)/shard_map/reduce_scatter | solution.py:35
  631.4 126.5 %reduce-scatter.23.cloned.1.call-start = ((), (), s32[]{:S(2)}) async-start(), calls=%async_computation.12 | async-start | bytes 884736
  636.6 159.8 %reduce-scatter.19.cloned.1.call-start = ((), (), s32[]{:S(2)}) async-start(), calls=%async_computation.10 | async-start | bytes 884736
  644.3 190.7 %reduce-scatter.21.cloned.1.call-start = ((), (), s32[]{:S(2)}) async-start(), calls=%async_computation.11 | async-start | bytes 884736
  (122 other events, 506.5 us)
Sparse Core Ops, SparseCore 0:
  89.2 121.7 all-reduce.15
  246.0 120.4 all-reduce.13
  395.3 120.4 all-reduce.11
  616.6 120.4 all-reduce.9
Sparse Core Ops, SparseCore 1:
  91.4 24.1 all-gather.2
  117.4 23.9 all-gather.4
  592.0 34.0 reduce-scatter.24
  630.0 42.3 reduce-scatter.16
  676.7 42.4 reduce-scatter.14
  722.9 34.9 reduce-scatter.22
  761.4 34.9 reduce-scatter.18
  800.0 34.9 reduce-scatter.20
where the time goes:
time: 849 us; the launch traced here: 842 us
  waiting for transfers between devices  507 us (60%)
  matrix products  153 us (18%)
  other arithmetic  75.2 us (9%)
  blocking collectives  65.8 us (8%)
  local copies, waits for them, and re-layouts  22.8 us (3%)
  between operations  17.1 us (2%)
    psum x1, waiting for transfers between devices, body(): lax.psum(contract_rows(mixed_cols, full_o).astype(jnp.bfloat16), 'tensor')  121 us
    psum x1, waiting for transfers between devices, body(): lax.psum(jnp.dot(hidden, full_second, preferred_element_type=jnp.float32)...  121 us
    psum x1, waiting for transfers between devices, body(): lax.psum(contract_cols(grad_inner, full_first).astype(jnp.bfloat16), 'ten...  121 us
    unnamed x16, waiting for transfers between devices  93 us
    psum x1, waiting for transfers between devices, body(): lax.psum(back_terms.astype(jnp.bfloat16), 'tensor').astype(jnp.float32)  52.3 us
    psum x1, blocking collectives, reduce_small(): lax.psum((grads[0], grads[1], grads[2], grads[3], grads[4], grads[5], gra...  26.5 us
    dot_general x12, matrix products, contract_cols(): lax.dot_general(left, right, (((1,), (1,)), ((), ())), preferred_element_...  21.3 us
    dot_general x2, matrix products, body(): jnp.dot(first_low, full_first, preferred_element_type=jnp.float32) + b1  21 us
  transfers between devices with their start and end apart: 12, of which 7 were waited for; matrix products, arithmetic and copies ran while one was open for 11% of the time, Pallas kernels for 0%

commit v1 on v0

--- a/solution.py
+++ b/solution.py
@@ -7,6 +7,11 @@
 HD = 64
 eps_norm = 1e-12
 masked_score = -1e30
+
+
+def update_plane(x0):
+    y = jnp.sum(lax.all_gather(x0, axis_name="tensor"), 0)
+    return y
 
 
 def doc_ids(lengths, count):
@@ -162,9 +167,9 @@
             )
             log_totals.append(log_total)
         mixed_cols = jnp.concatenate(pieces, axis=2).reshape(width, seq_len).astype(jnp.bfloat16)
-        attended = lax.psum(
-            contract_rows(mixed_cols, full_o).astype(jnp.bfloat16), "tensor"
-        ).astype(jnp.float32)
+        attended = update_plane(contract_rows(mixed_cols, full_o).astype(jnp.bfloat16)).astype(
+            jnp.float32
+        )
         first, normed_one, scaled_one = norm_forward(inputs + attended + bo, gain1, shift1)
         first_low = first.astype(jnp.bfloat16)
         inner = jnp.dot(first_low, full_first, preferred_element_type=jnp.float32) + b1

time: 849 us -> 1080 us (1.27)
  waiting for transfers between devices: 507 us -> 731 us
    all_gather x0 -> x2, waiting for transfers between devices: none -> 206 us  [update_plane(): y = jnp.sum(lax.all_gather(x0, axis_name='tensor'), 0)]
    psum x1 -> x0, waiting for transfers between devices: 121 us -> none  [body(): lax.psum(contract_rows(mixed_cols, full_o).astype(jnp.bfloat16), 'tensor')]
    reduce_scatter x1, waiting for transfers between devices: 0.01 us -> 46.7 us  [reduce_large(): lax.psum_scatter(grads[4], 'dp', scatter_dimension=0, tiled=True)]
    reduce_scatter x1, waiting for transfers between devices: 0.01 us -> 39.4 us  [reduce_large(): lax.psum_scatter(grads[5], 'dp', scatter_dimension=1, tiled=True)]
    unnamed x16 -> x17, waiting for transfers between devices: 93 us -> 117 us
    all_gather x1, waiting for transfers between devices: 0.01 us -> 13.6 us  [collect(): lax.all_gather(w1, 'dp', axis=0, tiled=True)]
    unnamed x290 -> x274, local copies, waits for them, and re-layouts: 20.9 us -> 21.8 us
  transfers between devices with their start and end apart: 12 -> 13, of which waited for: 7 -> 12; matrix products, arithmetic and copies ran while one was open for 11% -> 12% of each run, Pallas kernels for 0% -> 0%
where the time goes in v1:
time: 1080 us; the launch traced here: 1070 us
  waiting for transfers between devices  731 us (68%)
  matrix products  151 us (14%)
  other arithmetic  84.3 us (8%)
  blocking collectives  66.1 us (6%)
  local copies, waits for them, and re-layouts  23.9 us (2%)
  between operations  15.7 us (1%)
    all_gather x2, waiting for transfers between devices, update_plane(): y = jnp.sum(lax.all_gather(x0, axis_name='tensor'), 0)  206 us
    psum x1, waiting for transfers between devices, body(): lax.psum(jnp.dot(hidden, full_second, preferred_element_type=jnp.float32)...  121 us
    psum x1, waiting for transfers between devices, body(): lax.psum(contract_cols(grad_inner, full_first).astype(jnp.bfloat16), 'ten...  120 us
    unnamed x17, waiting for transfers between devices  117 us
    psum x1, waiting for transfers between devices, body(): lax.psum(back_terms.astype(jnp.bfloat16), 'tensor').astype(jnp.float32)  63 us
    reduce_scatter x1, waiting for transfers between devices, reduce_large(): lax.psum_scatter(grads[4], 'dp', scatter_dimension=0, tiled=True)  46.7 us
    reduce_scatter x1, waiting for transfers between devices, reduce_large(): lax.psum_scatter(grads[5], 'dp', scatter_dimension=1, tiled=True)  39.4 us
    psum x1, blocking collectives, reduce_small(): lax.psum((grads[0], grads[1], grads[2], grads[3], grads[4], grads[5], gra...  26.8 us
  transfers between devices with their start and end apart: 13, of which 12 were waited for; matrix products, arithmetic and copies ran while one was open for 12% of the time, Pallas kernels for 0%

profile of v1, /device:TPU:0, one launch (start us, length us, event | category | flops | bytes accessed | tf_op | source)
XLA Modules:
  0.0 1074.6 jit_solution(2197786599725825847)
XLA Ops:
  9.9 11.4 %all_gather.23 = bf16[192,768]{0,1:T(8,128)(2,1)S(1)} all-gather(bf16[192,96]{0,1:T(8,128)(2,1)} %copy.42), channel_id=1, replica_groups=mesh['dp'=8,'tensor'=4] {'dp'}, dimensions={1}, use_global_device_ids=true | all-gather | bytes 331776 | tf_op jit(solution)/shard_map/all_gather | solution.py:28
  21.3 9.3 all_gather.21
  30.6 8.8 all_gather.22
  39.5 9.8 all_gather.20
  86.4 95.9 %all-gather.13.cloned.1.call-done = bf16[4096,768]{1,0:T(8,128)(2,1)} async-done(((bf16[1024,768]{1,0:T(8,128)(2,1)}), bf16[4096,768]{1,0:T(8,128)(2,1)}) %all-gather.13.cloned.1.call-update) | async-done | bytes 6291472 | tf_op jit(solution)/shard_map/all_gather | solution.py:13
  182.3 5.3 reduce_sum.439
  187.6 110.5 %all-gather.11.cloned.1.call-done = bf16[4096,768]{1,0:T(8,128)(2,1)} async-done(((bf16[1024,768]{1,0:T(8,128)(2,1)}), bf16[4096,768]{1,0:T(8,128)(2,1)}) %all-gather.11.cloned.1.call-update) | async-done | bytes 6291472 | tf_op jit(solution)/shard_map/all_gather | solution.py:13
  298.1 5.3 reduce_sum.431
  308.7 13.6 %all-gather.7.cloned.1.call-done = bf16[768,768]{1,0:T(8,128)(2,1)} async-done(((bf16[96,768]{1,0:T(8,128)(2,1)}), bf16[768,768]{1,0:T(8,128)(2,1)}) %all-gather.7.cloned.1.call-update) | async-done | bytes 1179664 | tf_op jit(solution)/shard_map/all_gather | solution.py:29
  327.9 17.1 %multiply_convert_fusion.5 = (bf16[1024,768]{1,0:T(8,128)(2,1)}, f32[1024,768]{1,0:T(8,128)}, bf16[1024,768]{1,0:T(8,128)(2,1)}, f32[1024,768]{1,0:T(8,128)}, f32[1024,768]{1,0:T(8,128)}) fusion(f32[768]{0:T(1024)S(1)} %copy-done.110, f32[1024,768]{1,0:T(8,128)S(1)} %fusion.68, bf16[768,768]{1,0:T(8,128)(2,1)S(1)} %copy-done.106, f32[768]{0:T(1024)S(1)} %copy-done.102, ...), kind=kOutput, calls=%fused_computation.92 | convolution fusion | flops 1318846464 | bytes 20078592 | tf_op jit(solution)/shard_map/dot_general | solution.py:175
  348.1 4.4 convolution_convert_fusion.4
  355.7 121.1 %all-reduce.12.cloned.1.call-done = (bf16[1024,768]{1,0:T(8,128)(2,1)}, bf16[1024,768]{1,0:T(8,128)(2,1)}) async-done(((bf16[1024,768]{1,0:T(8,128)(2,1)}, bf16[1024,768]{1,0:T(8,128)(2,1)}), (bf16[1024,768]{1,0:T(8,128)(2,1)}, bf16[1024,768]{1,0:T(8,128)(2,1)})) %all-reduce.12.cloned.1.call-update) | async-done | bytes 3145744 | tf_op jit(solution)/shard_map/psum | solution.py:177
  476.8 5.0 fusion.131
  487.3 4.4 fusion.18
  505.4 120.4 %all-reduce.10.cloned.1.call-done = (bf16[1024,768]{1,0:T(8,128)(2,1)}, bf16[1024,768]{1,0:T(8,128)(2,1)}) async-done(((bf16[1024,768]{1,0:T(8,128)(2,1)}, bf16[1024,768]{1,0:T(8,128)(2,1)}), (bf16[1024,768]{1,0:T(8,128)(2,1)}, bf16[1024,768]{1,0:T(8,128)(2,1)})) %all-reduce.10.cloned.1.call-update) | async-done | bytes 3145744 | tf_op jit(solution)/shard_map/psum | solution.py:198
  625.8 9.2 multiply_reduce_fusion.5
  635.1 5.3 fusion.130
  647.1 4.4 multiply_reduce_fusion
  655.9 8.4 multiply_convert_fusion
  669.8 5.7 fusion.84
  675.6 4.5 multiply_reduce_fusion.2
  680.0 4.4 multiply_reduce_fusion.3
  684.4 8.2 multiply_convert_fusion.2
  702.2 5.8 convert_reduce_fusion.4
  708.0 5.6 convert_reduce_fusion.5
  768.4 26.8 %all-reduce = (f32[192]{0:T(256)}, f32[192]{0:T(256)}, f32[768]{0:T(1024)}, f32[768]{0:T(1024)}, f32[768]{0:T(1024)}, /*index=5*/f32[768]{0:T(1024)}, f32[768]{0:T(1024)}, f32[768]{0:T(1024)}, f32[768]{0:T(1024)}) all-reduce(f32[192]{0:T(256)} %reshape.373, f32[192]{0:T(256)} %reshape.374, ...), channel_id=1, replica_groups=mesh['dp'=8,'tensor'=4] {'dp'}, use_global_device_ids=true, to_apply=%region_43.44 | all-reduce | flops 5760 | bytes 46080 | tf_op jit(solution)/shard_map/psum | solution.py:46
  796.8 63.0 %all-reduce.8.cloned.1.call-done = (bf16[1024,768]{1,0:T(8,128)(2,1)}, bf16[1024,768]{1,0:T(8,128)(2,1)}) async-done(((bf16[1024,768]{1,0:T(8,128)(2,1)}, bf16[1024,768]{1,0:T(8,128)(2,1)}), (bf16[1024,768]{1,0:T(8,128)(2,1)}, bf16[1024,768]{1,0:T(8,128)(2,1)})) %all-reduce.8.cloned.1.call-update) | async-done | bytes 3145744 | tf_op jit(solution)/shard_map/psum | solution.py:255
  865.8 39.4 %reduce-scatter.17.cloned.1.call-done = f32[768,96]{0,1:T(8,128)} async-done(((f32[768,768]{0,1:T(8,128)}), f32[768,96]{0,1:T(8,128)}) %reduce-scatter.17.cloned.1.call-update) | async-done | bytes 294928 | tf_op jit(solution)/shard_map/reduce_scatter | solution.py:41
  905.2 46.7 %reduce-scatter.15.cloned.1.call-done = f32[96,768]{1,0:T(8,128)} async-done(((f32[768,768]{1,0:T(8,128)}), f32[96,768]{1,0:T(8,128)}) %reduce-scatter.15.cloned.1.call-update) | async-done | bytes 294928 | tf_op jit(solution)/shard_map/reduce_scatter | solution.py:40
  951.9 38.7 %reduce-scatter.23.cloned.1.call-done = f32[96,192]{1,0:T(8,128)} async-done(((f32[768,192]{1,0:T(8,128)}), f32[96,192]{1,0:T(8,128)}) %reduce-scatter.23.cloned.1.call-update) | async-done | bytes 73744
  990.6 38.6 %reduce-scatter.19.cloned.1.call-done = f32[96,192]{1,0:T(8,128)} async-done(((f32[768,192]{1,0:T(8,128)}), f32[96,192]{1,0:T(8,128)}) %reduce-scatter.19.cloned.1.call-update) | async-done | bytes 73744
  1029.2 38.7 %reduce-scatter.21.cloned.1.call-done = f32[96,192]{1,0:T(8,128)} async-done(((f32[768,192]{1,0:T(8,128)}), f32[96,192]{1,0:T(8,128)}) %reduce-scatter.21.cloned.1.call-update) | async-done | bytes 73744
  (416 shorter events, 163.3 us)
Async XLA Ops:
  7.2 44.3 %copy-start = (bf16[2048,768]{1,0:T(8,128)(2,1)S(1)}, bf16[2048,768]{1,0:T(8,128)(2,1)}, u32[]{:S(2)}) copy-start(bf16[2048,768]{1,0:T(8,128)(2,1)} %param.18) | copy-start | bytes 9437188
  7.2 175.1 %all-gather.13.cloned.1.call-start = ((), (), s32[]{:S(2)}) async-start(), calls=%async_computation.9 | async-start | bytes 7864320 | tf_op jit(solution)/shard_map/all_gather | solution.py:13
  9.9 41.6 %copy-start.112 = (f32[192]{0:T(256)S(1)}, f32[192]{0:T(256)}, u32[]{:S(2)}) copy-start(f32[192]{0:T(256)} %param.21) | copy-start | bytes 2308
  30.6 21.7 %copy-start.48 = (bf16[768,192]{1,0:T(8,128)(2,1)}, bf16[768,192]{1,0:T(8,128)(2,1)S(1)}, u32[]{:S(2)}) copy-start(bf16[768,192]{1,0:T(8,128)(2,1)S(1)} %all_gather.21) | copy-start | bytes 884740
  39.4 13.5 %copy-start.50 = (bf16[768,192]{1,0:T(8,128)(2,1)}, bf16[768,192]{1,0:T(8,128)(2,1)S(1)}, u32[]{:S(2)}) copy-start(bf16[768,192]{1,0:T(8,128)(2,1)S(1)} %all_gather.22) | copy-start | bytes 884740
  49.3 10.0 copy-start.40
  66.5 231.6 %all-gather.11.cloned.1.call-start = ((), (), s32[]{:S(2)}) async-start(), calls=%async_computation.8 | async-start | bytes 7864320 | tf_op jit(solution)/shard_map/all_gather | solution.py:13
  84.8 237.5 %all-gather.7.cloned.1.call-start = ((), (), s32[]{:S(2)}) async-start(), calls=%async_computation.6 | async-start | bytes 1327104 | tf_op jit(solution)/shard_map/all_gather | solution.py:29
  85.6 262.6 %all-gather.9.cloned.1.call-start = ((), (), s32[]{:S(2)}) async-start(), calls=%async_computation.7 | async-start | bytes 1327104 | tf_op jit(solution)/shard_map/all_gather | solution.py:30
  86.2 390.7 %all-reduce.12.cloned.1.call-start = ((), (), s32[]{:S(2)}) async-start(), calls=%async_computation.18 | async-start | bytes 6291456 | tf_op jit(solution)/shard_map/psum | solution.py:177
  355.2 270.5 %all-reduce.10.cloned.1.call-start = ((), (), s32[]{:S(2)}) async-start(), calls=%async_computation.17 | async-start | bytes 6291456 | tf_op jit(solution)/shard_map/psum | solution.py:198
  505.1 290.0 %reduce-scatter.25.cloned.1.call-start = ((), (), s32[]{:S(2)}) async-start(), calls=%async_computation.15 | async-start | bytes 884736
  625.7 9.2 copy-start.6
  625.7 9.2 copy-start.10
  625.8 9.3 copy-start.16
  625.8 9.3 copy-start.19
  625.8 9.3 copy-start.39
  625.8 9.3 copy-start.85
  625.8 9.3 copy-start.88
  625.8 18.4 %slice-start.2 = ((s8[6291456]{0:T(1024)(128)(4,1)}), s8[4194304]{0:T(1024)(128)(4,1)S(1)}, s32[]{:S(2)}) async-start(s8[6291456]{0:T(1024)(128)(4,1)} %bitcast.113), calls=%async_computation.21 | async-start | bytes 8388608
  655.9 12.2 %copy-start.57 = (bf16[192,1024]{1,0:T(8,128)(2,1)S(1)}, bf16[192,1024]{1,0:T(8,128)(2,1)}, u32[]{:S(2)}) copy-start(bf16[192,1024]{1,0:T(8,128)(2,1)} %copy-done.56) | copy-start | bytes 1179652
  655.9 13.9 %copy-start.84 = (f32[3,512]{1,0:T(4,128)S(1)}, f32[3,512]{1,0:T(4,128)}, u32[]{:S(2)}) copy-start(f32[3,512]{1,0:T(4,128)} %copy-done.83) | copy-start | bytes 18436
  664.3 11.2 %slice-start.4 = ((s8[6291456]{0:T(1024)(128)(4,1)}), s8[4194304]{0:T(1024)(128)(4,1)S(1)}, s32[]{:S(2)}) async-start(s8[6291456]{0:T(1024)(128)(4,1)} %bitcast.115), calls=%async_computation.23 | async-start | bytes 8388608
  669.8 10.3 slice-start.6
  701.7 158.1 %all-reduce.8.cloned.1.call-start = ((), (), s32[]{:S(2)}) async-start(), calls=%async_computation.16 | async-start | bytes 6291456 | tf_op jit(solution)/shard_map/psum | solution.py:255
  708.0 14.6 %copy-start.55 = (bf16[3,64,1024]{2,1,0:T(8,128)(2,1)}, bf16[3,64,1024]{2,1,0:T(8,128)(2,1)S(1)}, u32[]{:S(2)}) copy-start(bf16[3,64,1024]{2,1,0:T(8,128)(2,1)S(1)} %get-tuple-element.174) | copy-start | bytes 1179652
  713.6 10.8 %copy-start.74 = (bf16[3,64,1024]{2,1,0:T(8,128)(2,1)}, bf16[3,64,1024]{2,1,0:T(8,128)(2,1)S(1)}, u32[]{:S(2)}) copy-start(bf16[3,64,1024]{2,1,0:T(8,128)(2,1)S(1)} %get-tuple-element.172) | copy-start | bytes 1179652
  726.2 179.0 %reduce-scatter.17.cloned.1.call-start = ((), (), s32[]{:S(2)}) async-start(), calls=%async_computation.11 | async-start | bytes 2654208 | tf_op jit(solution)/shard_map/reduce_scatter | solution.py:41
  733.5 218.4 %reduce-scatter.15.cloned.1.call-start = ((), (), s32[]{:S(2)}) async-start(), calls=%async_computation.10 | async-start | bytes 2654208 | tf_op jit(solution)/shard_map/reduce_scatter | solution.py:40
  741.2 249.4 %reduce-scatter.23.cloned.1.call-start = ((), (), s32[]{:S(2)}) async-start(), calls=%async_computation.14 | async-start | bytes 884736
  747.5 281.7 %reduce-scatter.19.cloned.1.call-start = ((), (), s32[]{:S(2)}) async-start(), calls=%async_computation.12 | async-start | bytes 884736
  756.1 311.8 %reduce-scatter.21.cloned.1.call-start = ((), (), s32[]{:S(2)}) async-start(), calls=%async_computation.13 | async-start | bytes 884736
  (115 other events, 472.3 us)
Sparse Core Ops, SparseCore 0:
  66.6 115.6 all-gather.12
  184.5 113.5 all-gather.10
  300.0 22.2 all-gather.6
  324.0 24.0 all-gather.8
  355.3 121.4 all-reduce.11
  505.3 120.4 all-reduce.9
  701.8 34.0 reduce-scatter.24
  738.3 121.4 all-reduce.7
  863.7 41.5 reduce-scatter.16
  909.4 42.4 reduce-scatter.14
  955.6 34.9 reduce-scatter.22
  994.2 34.9 reduce-scatter.18
  1032.9 34.9 reduce-scatter.20
